TPU v7x, 32 devices: a whole 2x2x4 slice. The times are simulated.
32 devices in a mesh: tiles: 8 (over z, y), rhs: 4 (over x, core).
Axes of the slice: x: 2, y: 2, z: 4, core: 2. Of those that a mesh axis runs over, the one named last changes fastest.
Arguments:
- rhs_rows: bfloat16 [256, 8192], P('rhs', 'tiles'), may hold values from -6 to 6
- diag_inverse: bfloat16 [8192, 1024], P('tiles', 'rhs'), may hold values from -0.0625 to 0.5625
- u_factors: bfloat16 [8, 7, 1024, 128], P('tiles'), may hold values from -0.1875 to 0.1875
- v_factors: bfloat16 [8, 7, 1024, 128], P('tiles'), may hold values from -0.1875 to 0.1875
- tile_rows: int32 [8, 7], P('tiles'), may hold values from 0 to 7, as said below
- tile_ranks: int32 [8, 7], P('tiles'), may hold values from 16 to 128
- point_coords: float32 [8, 8192], P(None, 'tiles'), may hold values from 0 to 1
- cand_coords: float32 [8, 128], P(None, 'rhs'), may hold values from 0 to 1
- owner: int32 [128], P('rhs'), may hold values from 0 to 7, as said below
Outputs:
- solution: bfloat16 [256, 8192], P('rhs', 'tiles')
- predictions: float32 [128, 256], P(('tiles', 'rhs'))
Inputs may be any that keep to these rules, and one draw needn't show every extreme that they name: Each tile column lists 7 distinct tile rows, none equal to itself; for each slot k, tile_rows[., k] is a permutation of the tile rows. `owner`: in each group of 32 consecutive candidates every tile owns exactly 4.
All inputs are finite; a program needn't handle non-finite values.
Results may differ from a plain program's by a relative error of at most 0.008.
Values may be sent and summed in bfloat16 or wider, within the bound.
No kernel may reach another device: no remote copies, remote signals or barrier semaphores. Data moves between devices by JAX's collectives and lax.ppermute only.
A program may use at most 64 MiB of HBM per device.

v0:
```python
import math
import jax
import jax.numpy as jnp
from jax import lax
from jax.sharding import PartitionSpec as P

ITERS = 2


def kernel_block(cand, cand_sq, points, amplitude):
    point_sq = jnp.sum(points * points, 0)
    inner_products = lax.dot_general(
        cand, points, (((0,), (0,)), ((), ())), precision=lax.Precision.HIGHEST
    )
    dist_sq = cand_sq[:, None] + point_sq[None, :] - 2.0 * inner_products
    return (jnp.exp(-2.0 * dist_sq) * amplitude).astype(jnp.bfloat16)


def per_device(
    rhs_rows,
    diag_inverse,
    u_factors,
    v_factors,
    tile_rows,
    tile_ranks,
    point_coords,
    cand_coords,
    owner,
):
    tiles_count = lax.axis_size("tiles")
    tile_here = lax.axis_index("tiles")
    u_slots = u_factors[0]
    v_slots = v_factors[0]
    width = u_slots.shape[2]
    slot_count = u_slots.shape[0]
    rank_mask = (
        lax.broadcasted_iota(jnp.int32, (slot_count, width), 1) < tile_ranks[0][:, None]
    ).astype(jnp.bfloat16)
    peer_ids = jnp.arange(tiles_count, dtype=jnp.int32)
    all_rows = lax.all_gather(tile_rows, "tiles", axis=0, tiled=True)
    slot_range = jnp.arange(slot_count, dtype=jnp.int32)
    column_ids = jnp.broadcast_to(peer_ids[:, None], all_rows.shape)
    all_sources = (
        jnp.zeros(all_rows.shape, jnp.int32).at[all_rows, slot_range[None, :]].set(column_ids)
    )
    sources_here = lax.dynamic_slice_in_dim(all_sources, tile_here, 1, 0)[0]
    to_rows = (peer_ids[:, None] == tile_rows[0][None, :]).astype(jnp.bfloat16)
    to_cols = (peer_ids[:, None] == sources_here[None, :]).astype(jnp.bfloat16)
    whole_inverse = lax.all_gather(diag_inverse, "rhs", axis=1, tiled=True)

    def precondition(resid):
        return jnp.dot(resid, whole_inverse, preferred_element_type=jnp.float32).astype(
            jnp.bfloat16
        )

    iterate = precondition(rhs_rows)
    for sweep in range(ITERS):
        lower = jnp.einsum("cb,kbr->kcr", iterate, v_slots, preferred_element_type=jnp.float32)
        lower = (lower * rank_mask[:, None, :]).astype(jnp.bfloat16)
        upper = jnp.einsum(
            "cb,kbr->kcr", iterate, u_slots, preferred_element_type=jnp.float32
        ).astype(jnp.bfloat16)
        send_lower = jnp.einsum(
            "nk,kcr->ncr", to_rows, lower, preferred_element_type=jnp.float32
        ).astype(jnp.bfloat16)
        send_upper = jnp.einsum(
            "nk,kcr->ncr", to_cols, upper, preferred_element_type=jnp.float32
        ).astype(jnp.bfloat16)
        from_picked = jnp.einsum(
            "nk,ncr->kcr",
            to_cols,
            lax.all_to_all(send_lower, "tiles", split_axis=0, concat_axis=0, tiled=True),
            preferred_element_type=jnp.float32,
        ).astype(jnp.bfloat16)
        first = jnp.einsum("kcr,kbr->cb", from_picked, u_slots, preferred_element_type=jnp.float32)
        picked = jnp.einsum(
            "nk,ncr->kcr",
            to_rows,
            lax.all_to_all(send_upper, "tiles", split_axis=0, concat_axis=0, tiled=True),
            preferred_element_type=jnp.float32,
        ).astype(jnp.bfloat16)
        picked = picked * rank_mask[:, None, :]
        second = jnp.einsum("kcr,kbr->cb", picked, v_slots, preferred_element_type=jnp.float32)
        resid = (rhs_rows.astype(jnp.float32) - (first + second)).astype(jnp.bfloat16)
        iterate = precondition(resid)
    block_len = u_slots.shape[1]
    amplitude = 4.0 / math.sqrt(block_len * tiles_count)
    cand_sq = jnp.sum(cand_coords * cand_coords, 0)
    cross = kernel_block(cand_coords, cand_sq, point_coords, amplitude)
    partial_values = lax.dot_general(
        cross,
        lax.all_gather(iterate, "rhs", axis=0, tiled=True),
        (((1,), (1,)), ((), ())),
        preferred_element_type=jnp.float32,
    )
    group_len = owner.shape[0]
    owned = group_len // tiles_count
    owner_hot = (owner[:, None] == peer_ids[None, :]).astype(jnp.int32)
    running = jnp.cumsum(owner_hot, axis=0)
    slot_of = owner * owned + jnp.sum(running * owner_hot, axis=1) - 1
    ordered = jnp.zeros_like(partial_values).at[slot_of].set(partial_values)
    summed = lax.psum(ordered, "tiles")
    owned_sums = lax.dynamic_slice_in_dim(summed, tile_here * owned, owned, 0)
    return (iterate, owned_sums)


def solution(mesh):
    in_specs = (
        P("rhs", "tiles"),
        P("tiles", "rhs"),
        P("tiles", None, None, None),
        P("tiles", None, None, None),
        P("tiles", None),
        P("tiles", None),
        P(None, "tiles"),
        P(None, "rhs"),
        P("rhs"),
    )
    out_specs = (P("rhs", "tiles"), P(("tiles", "rhs"), None))
    return jax.shard_map(
        per_device, mesh=mesh, in_specs=in_specs, out_specs=out_specs, check_vma=False
    )
```

profile of v0, /device:TPU:0, one launch (start us, length us, event | category | flops | bytes accessed | tf_op | source)
XLA Modules:
  0.0 142.5 jit_solution(6352598870871334731)
XLA Ops:
  7.2 0.7 all-gather.3.cloned.1.call-update
  7.9 22.5 %all-gather = s32[8,1,7]{2,1,0:T(1,128)S(1)} all-gather(s32[1,1,7]{2,1,0:T(1,128)} %bitcast.143), channel_id=1, replica_groups=mesh['tiles'=8,'rhs'=4] {'tiles'}, dimensions={0}, use_global_device_ids=true | all-gather | bytes 252 | tf_op jit(solution)/shard_map/all_gather | solution.py:40
  30.6 0.7 fusion.107
  31.4 3.5 %scatter_fusion = s32[8,7]{1,0:T(8,128)S(1)} fusion(s32[8,7]{1,0:T(8,128)S(1)} %broadcast.30, s32[56]{0:T(128)S(1)} %reshape.46, s32[56]{0:T(128)S(1)} %reshape.48), kind=kCustom, calls=%fused_computation | custom fusion | bytes 1120 | tf_op jit(solution)/shard_map/scatter | solution.py:44
  35.6 2.2 %fusion.71 = bf16[64,1024,1]{1,0,2:T(8,128)(2,1)S(1)} fusion(bf16[64,1024]{1,0:T(8,128)(2,1)S(1)} %copy-done.2, bf16[1024,1024]{1,0:T(8,128)(2,1)} %all-gather.3.cloned.1.call-done), kind=kOutput, calls=%fused_computation.46 | convolution fusion | flops 134283264 | bytes 2359296 | tf_op jit(solution)/shard_map/dot_general | solution.py:52
  38.5 0.7 copy.30
  39.2 5.0 %all-to-all-start.1 = ((bf16[8,64,128]{2,1,0:T(8,128)(2,1)}), bf16[8,64,128]{2,1,0:T(8,128)(2,1)S(1)}, u32[]{:S(2)}, u32[]{:S(2)}) async-start(bf16[8,64,128]{2,1,0:T(8,128)(2,1)} %copy.30), calls=%async_computation.1 | async-start | bytes 262144 | tf_op jit(solution)/shard_map/all_to_all | solution.py:79
  44.9 0.7 copy.25
  45.6 6.0 %all-to-all-done.1 = bf16[8,64,128]{2,1,0:T(8,128)(2,1)S(1)} async-done(((bf16[8,64,128]{2,1,0:T(8,128)(2,1)}), bf16[8,64,128]{2,1,0:T(8,128)(2,1)S(1)}, u32[]{:S(2)}, u32[]{:S(2)}) %all-to-all-start.1) | async-done | bytes 131104 | tf_op jit(solution)/shard_map/all_to_all | solution.py:79
  51.6 3.4 %all-to-all-start = ((bf16[8,64,128]{2,1,0:T(8,128)(2,1)}), bf16[8,64,128]{2,1,0:T(8,128)(2,1)S(1)}, u32[]{:S(2)}, u32[]{:S(2)}) async-start(bf16[8,64,128]{2,1,0:T(8,128)(2,1)} %copy.25), calls=%async_computation | async-start | bytes 262144 | tf_op jit(solution)/shard_map/all_to_all | solution.py:72
  55.9 6.4 %all-to-all-done = bf16[8,64,128]{2,1,0:T(8,128)(2,1)S(1)} async-done(((bf16[8,64,128]{2,1,0:T(8,128)(2,1)}), bf16[8,64,128]{2,1,0:T(8,128)(2,1)S(1)}, u32[]{:S(2)}, u32[]{:S(2)}) %all-to-all-start) | async-done | bytes 131104 | tf_op jit(solution)/shard_map/all_to_all | solution.py:72
  62.5 3.2 %fusion.68 = bf16[64,1024,1]{1,0,2:T(8,128)(2,1)S(1)} fusion(bf16[1024,1024]{1,0:T(8,128)(2,1)} %all-gather.3.cloned.1.call-done, f32[64,1024]{1,0:T(8,128)S(1)} %fusion.16, bf16[1,7,1024,128]{3,2,1,0:T(8,128)(2,1)} %param.11, bf16[64,1024]{1,0:T(8,128)(2,1)S(1)} %copy-done.2, bf16[7,64,128]{2,0,1:T(8,128)(2,1)S(1)} %convolution_convert_fusion.9), kind=kOutput, calls=%fused_computation.45 | convolution fusion | flops 251985920 | bytes 4571136 | tf_op jit(solution)/shard_map/dot_general | solution.py:52
  65.7 1.9 %fusion.84 = bf16[7,64,128]{2,1,0:T(8,128)(2,1)S(1)} fusion(bf16[64,1024,1]{1,0,2:T(8,128)(2,1)S(1)} %fusion.68, bf16[1,7,1024,128]{3,2,1,0:T(8,128)(2,1)} %param.11), kind=kOutput, calls=%fused_computation.56 | convolution fusion | flops 117497856 | bytes 2080768 | tf_op jit(solution)/shard_map/cb,kbr->kcr/dot_general | solution.py:60
  68.2 0.7 copy.40
  68.9 3.4 %all-to-all-start.3 = ((bf16[8,64,128]{2,1,0:T(8,128)(2,1)}), bf16[8,64,128]{2,1,0:T(8,128)(2,1)S(1)}, u32[]{:S(2)}, u32[]{:S(2)}) async-start(bf16[8,64,128]{2,1,0:T(8,128)(2,1)} %copy.40), calls=%async_computation.3 | async-start | bytes 262144 | tf_op jit(solution)/shard_map/all_to_all | solution.py:79
  72.6 0.7 copy.35
  73.3 6.3 %all-to-all-done.3 = bf16[8,64,128]{2,1,0:T(8,128)(2,1)S(1)} async-done(((bf16[8,64,128]{2,1,0:T(8,128)(2,1)}), bf16[8,64,128]{2,1,0:T(8,128)(2,1)S(1)}, u32[]{:S(2)}, u32[]{:S(2)}) %all-to-all-start.3) | async-done | bytes 131104 | tf_op jit(solution)/shard_map/all_to_all | solution.py:79
  79.6 3.4 %all-to-all-start.2 = ((bf16[8,64,128]{2,1,0:T(8,128)(2,1)}), bf16[8,64,128]{2,1,0:T(8,128)(2,1)S(1)}, u32[]{:S(2)}, u32[]{:S(2)}) async-start(bf16[8,64,128]{2,1,0:T(8,128)(2,1)} %copy.35), calls=%async_computation.2 | async-start | bytes 262144 | tf_op jit(solution)/shard_map/all_to_all | solution.py:72
  83.2 0.7 fusion.19
  83.9 6.4 %all-to-all-done.2 = bf16[8,64,128]{2,1,0:T(8,128)(2,1)S(1)} async-done(((bf16[8,64,128]{2,1,0:T(8,128)(2,1)}), bf16[8,64,128]{2,1,0:T(8,128)(2,1)S(1)}, u32[]{:S(2)}, u32[]{:S(2)}) %all-to-all-start.2) | async-done | bytes 131104 | tf_op jit(solution)/shard_map/all_to_all | solution.py:72
  90.5 3.2 %convolution_convert_fusion = bf16[64,1024]{1,0:T(8,128)(2,1)S(1)} fusion(bf16[1024,1024]{1,0:T(8,128)(2,1)} %all-gather.3.cloned.1.call-done, f32[64,1024]{1,0:T(8,128)S(1)} %fusion.19, bf16[1,7,1024,128]{3,2,1,0:T(8,128)(2,1)} %param.11, bf16[64,1024]{1,0:T(8,128)(2,1)S(1)} %copy-done.2, bf16[7,64,128]{2,0,1:T(8,128)(2,1)S(1)} %convolution_convert_fusion.5), kind=kOutput, calls=%fused_computation.30 | convolution fusion | flops 251985920 | bytes 4571136 | tf_op jit(solution)/shard_map/dot_general | solution.py:52
  93.7 6.5 %all_gather.11 = bf16[256,1024]{1,0:T(8,128)(2,1)S(1)} all-gather(bf16[64,1024]{1,0:T(8,128)(2,1)S(1)} %convolution_convert_fusion), channel_id=1, replica_groups=mesh['tiles'=8,'rhs'=4] {'rhs'}, dimensions={0}, use_global_device_ids=true | all-gather | bytes 655360 | tf_op jit(solution)/shard_map/all_gather | solution.py:92
  100.4 0.7 scatter_custom_fusion.1
  101.2 33.9 %psum.7 = f32[32,256]{1,0:T(8,128)S(1)} all-reduce(f32[32,256]{1,0:T(8,128)S(1)} %scatter_custom_fusion.1), channel_id=1, replica_groups=mesh['tiles'=8,'rhs'=4] {'tiles'}, use_global_device_ids=true, to_apply=%region_6.7 | all-reduce | flops 8192 | bytes 65536 | tf_op jit(solution)/shard_map/psum | solution.py:102
  (47 shorter events, 5.6 us)
Async XLA Ops:
  7.2 37.0 %copy-start = (bf16[1,7,1024,128]{3,2,1,0:T(8,128)(2,1)S(1)}, bf16[1,7,1024,128]{3,2,1,0:T(8,128)(2,1)}, u32[]{:S(2)}) copy-start(bf16[1,7,1024,128]{3,2,1,0:T(8,128)(2,1)} %param.12) | copy-start | bytes 5505028
  7.2 28.4 %all-gather.3.cloned.1.call-start = ((), (), s32[]{:S(2)}) async-start(), calls=%async_computation.4 | async-start | bytes 2621440 | tf_op jit(solution)/shard_map/all_gather | solution.py:49
  31.4 3.5 %copy-start.6 = (f32[8,32]{1,0:T(8,128)S(1)}, f32[8,32]{1,0:T(8,128)}, u32[]{:S(2)}) copy-start(f32[8,32]{1,0:T(8,128)} %param.16) | copy-start | bytes 3076
  31.4 3.6 %copy-start.4 = (f32[8,1024]{1,0:T(8,128)S(1)}, f32[8,1024]{1,0:T(8,128)}, u32[]{:S(2)}) copy-start(f32[8,1024]{1,0:T(8,128)} %param.15) | copy-start | bytes 98308
  31.4 3.6 %copy-start.7 = (s32[32]{0:T(128)S(1)}, s32[32]{0:T(128)}, u32[]{:S(2)}) copy-start(s32[32]{0:T(128)} %param.17) | copy-start | bytes 388
  31.4 3.8 %copy-start.8 = (s32[1,7]{1,0:T(1,128)S(1)}, s32[1,7]{1,0:T(1,128)}, u32[]{:S(2)}) copy-start(s32[1,7]{1,0:T(1,128)} %param.14) | copy-start | bytes 88
  31.4 4.2 %copy-start.2 = (bf16[64,1024]{1,0:T(8,128)(2,1)S(1)}, bf16[64,1024]{1,0:T(8,128)(2,1)}, u32[]{:S(2)}) copy-start(bf16[64,1024]{1,0:T(8,128)(2,1)} %param.9) | copy-start | bytes 393220
  35.6 2.2 %copy-start.1 = (bf16[1,7,1024,128]{3,2,1,0:T(8,128)(2,1)S(1)}, bf16[1,7,1024,128]{3,2,1,0:T(8,128)(2,1)}, u32[]{:S(2)}) copy-start(bf16[1,7,1024,128]{3,2,1,0:T(8,128)(2,1)} %param.11) | copy-start | bytes 5505028
  38.3 6.3 %copy-start.5 = (s32[1,7]{1,0:T(1,128)S(1)}, s32[1,7]{1,0:T(1,128)}, u32[]{:S(2)}) copy-start(s32[1,7]{1,0:T(1,128)} %param.13) | copy-start | bytes 88
  39.2 12.4 %all-to-all-start.1 = ((bf16[8,64,128]{2,1,0:T(8,128)(2,1)}), bf16[8,64,128]{2,1,0:T(8,128)(2,1)S(1)}, u32[]{:S(2)}, u32[]{:S(2)}) async-start(bf16[8,64,128]{2,1,0:T(8,128)(2,1)} %copy.30), calls=%async_computation.1 | async-start | bytes 262144 | tf_op jit(solution)/shard_map/all_to_all | solution.py:79
  51.6 10.7 %all-to-all-start = ((bf16[8,64,128]{2,1,0:T(8,128)(2,1)}), bf16[8,64,128]{2,1,0:T(8,128)(2,1)S(1)}, u32[]{:S(2)}, u32[]{:S(2)}) async-start(bf16[8,64,128]{2,1,0:T(8,128)(2,1)} %copy.25), calls=%async_computation | async-start | bytes 262144 | tf_op jit(solution)/shard_map/all_to_all | solution.py:72
  68.9 10.7 %all-to-all-start.3 = ((bf16[8,64,128]{2,1,0:T(8,128)(2,1)}), bf16[8,64,128]{2,1,0:T(8,128)(2,1)S(1)}, u32[]{:S(2)}, u32[]{:S(2)}) async-start(bf16[8,64,128]{2,1,0:T(8,128)(2,1)} %copy.40), calls=%async_computation.3 | async-start | bytes 262144 | tf_op jit(solution)/shard_map/all_to_all | solution.py:79
  79.6 10.7 %all-to-all-start.2 = ((bf16[8,64,128]{2,1,0:T(8,128)(2,1)}), bf16[8,64,128]{2,1,0:T(8,128)(2,1)S(1)}, u32[]{:S(2)}, u32[]{:S(2)}) async-start(bf16[8,64,128]{2,1,0:T(8,128)(2,1)} %copy.35), calls=%async_computation.2 | async-start | bytes 262144 | tf_op jit(solution)/shard_map/all_to_all | solution.py:72
  93.7 42.0 %copy-start.3 = (bf16[64,1024]{1,0:T(8,128)(2,1)}, bf16[64,1024]{1,0:T(8,128)(2,1)S(1)}, u32[]{:S(2)}) copy-start(bf16[64,1024]{1,0:T(8,128)(2,1)S(1)} %convolution_convert_fusion) | copy-start | bytes 393220
Sparse Core Ops, SparseCore 0:
  9.5 25.5 all-gather.2
where the time goes:
time: 143 us
  blocking collectives  62.9 us (44%)
  waiting for transfers between devices  25.7 us (18%)
  matrix products  15.6 us (11%)
  starting transfers between devices  15.1 us (11%)
  between operations  14.4 us (10%)
  local copies, waits for them, and re-layouts  7.77 us (5%)
    psum x1, blocking collectives, per_device(): summed = lax.psum(ordered, 'tiles')  33.9 us
    all_gather x1, blocking collectives, per_device(): all_rows = lax.all_gather(tile_rows, 'tiles', axis=0, tiled=True)  22.5 us
    all_to_all x2, waiting for transfers between devices, per_device(): lax.all_to_all(send_lower, 'tiles', split_axis=0, concat_axis=0, tiled=True)  12.7 us
    all_to_all x2, waiting for transfers between devices, per_device(): lax.all_to_all(send_upper, 'tiles', split_axis=0, concat_axis=0, tiled=True)  12.2 us
    dot_general x3, matrix products, precondition(): jnp.dot(resid, whole_inverse, preferred_element_type=jnp.float32)  8.6 us
    all_to_all x2, starting transfers between devices, per_device(): lax.all_to_all(send_upper, 'tiles', split_axis=0, concat_axis=0, tiled=True)  8.37 us
    all_to_all x2, starting transfers between devices, per_device(): lax.all_to_all(send_lower, 'tiles', split_axis=0, concat_axis=0, tiled=True)  6.74 us
    all_gather x1, blocking collectives, per_device(): lax.all_gather(iterate, 'rhs', axis=0, tiled=True)  6.5 us
  transfers between devices with their start and end apart: 5, of which 4 were waited for; matrix products, arithmetic and copies ran while one was open for 6% of the time, Pallas kernels for 0%

commit v1 on v0

--- a/solution.py
+++ b/solution.py
@@ -99,7 +99,7 @@
     running = jnp.cumsum(owner_hot, axis=0)
     slot_of = owner * owned + jnp.sum(running * owner_hot, axis=1) - 1
     ordered = jnp.zeros_like(partial_values).at[slot_of].set(partial_values)
-    summed = lax.psum(ordered, "tiles")
+    summed = jnp.sum(lax.all_gather(ordered, "tiles"), axis=0)
     owned_sums = lax.dynamic_slice_in_dim(summed, tile_here * owned, owned, 0)
     return (iterate, owned_sums)
 

time: 143 us -> 140 us (0.979)
  blocking collectives: 62.9 us -> 59.8 us
    psum x1 -> x0, blocking collectives: 33.9 us -> none  [per_device(): summed = lax.psum(ordered, 'tiles')]
    all_gather x0 -> x1, blocking collectives: none -> 30.9 us  [per_device(): summed = jnp.sum(lax.all_gather(ordered, 'tiles'), axis=0)]
  transfers between devices with their start and end apart: 5 -> 5, of which waited for: 4 -> 4; matrix products, arithmetic and copies ran while one was open for 6% -> 7% of each run, Pallas kernels for 0% -> 0%
where the time goes in v1:
time: 140 us
  blocking collectives  59.8 us (43%)
  waiting for transfers between devices  25.7 us (18%)
  matrix products  15.6 us (11%)
  starting transfers between devices  15.1 us (11%)
  between operations  14.4 us (10%)
  local copies, waits for them, and re-layouts  7.77 us (6%)
    all_gather x1, blocking collectives, per_device(): summed = jnp.sum(lax.all_gather(ordered, 'tiles'), axis=0)  30.9 us
    all_gather x1, blocking collectives, per_device(): all_rows = lax.all_gather(tile_rows, 'tiles', axis=0, tiled=True)  22.5 us
    all_to_all x2, waiting for transfers between devices, per_device(): lax.all_to_all(send_lower, 'tiles', split_axis=0, concat_axis=0, tiled=True)  12.7 us
    all_to_all x2, waiting for transfers between devices, per_device(): lax.all_to_all(send_upper, 'tiles', split_axis=0, concat_axis=0, tiled=True)  12.2 us
    dot_general x3, matrix products, precondition(): jnp.dot(resid, whole_inverse, preferred_element_type=jnp.float32)  8.6 us
    all_to_all x2, starting transfers between devices, per_device(): lax.all_to_all(send_upper, 'tiles', split_axis=0, concat_axis=0, tiled=True)  8.37 us
    all_to_all x2, starting transfers between devices, per_device(): lax.all_to_all(send_lower, 'tiles', split_axis=0, concat_axis=0, tiled=True)  6.74 us
    all_gather x1, blocking collectives, per_device(): lax.all_gather(iterate, 'rhs', axis=0, tiled=True)  6.5 us
  transfers between devices with their start and end apart: 5, of which 4 were waited for; matrix products, arithmetic and copies ran while one was open for 7% of the time, Pallas kernels for 0%

profile of v1, /device:TPU:0, one launch (start us, length us, event | category | flops | bytes accessed | tf_op | source)
XLA Modules:
  0.0 139.5 jit_solution(9370438221219623401)
XLA Ops:
  7.2 0.7 all-gather.4.cloned.1.call-update
  7.9 22.5 %all-gather.1 = s32[8,1,7]{2,1,0:T(1,128)S(1)} all-gather(s32[1,1,7]{2,1,0:T(1,128)} %bitcast.145), channel_id=1, replica_groups=mesh['tiles'=8,'rhs'=4] {'tiles'}, dimensions={0}, use_global_device_ids=true | all-gather | bytes 252 | tf_op jit(solution)/shard_map/all_gather | solution.py:40
  30.6 0.7 fusion.107
  31.4 3.5 %scatter_fusion = s32[8,7]{1,0:T(8,128)S(1)} fusion(s32[8,7]{1,0:T(8,128)S(1)} %broadcast.30, s32[56]{0:T(128)S(1)} %reshape.46, s32[56]{0:T(128)S(1)} %reshape.48), kind=kCustom, calls=%fused_computation | custom fusion | bytes 1120 | tf_op jit(solution)/shard_map/scatter | solution.py:44
  35.6 2.2 %fusion.71 = bf16[64,1024,1]{1,0,2:T(8,128)(2,1)S(1)} fusion(bf16[64,1024]{1,0:T(8,128)(2,1)S(1)} %copy-done.2, bf16[1024,1024]{1,0:T(8,128)(2,1)} %all-gather.4.cloned.1.call-done), kind=kOutput, calls=%fused_computation.46 | convolution fusion | flops 134283264 | bytes 2359296 | tf_op jit(solution)/shard_map/dot_general | solution.py:52
  38.5 0.7 copy.50
  39.2 5.0 %all-to-all-start.1 = ((bf16[8,64,128]{2,1,0:T(8,128)(2,1)}), bf16[8,64,128]{2,1,0:T(8,128)(2,1)S(1)}, u32[]{:S(2)}, u32[]{:S(2)}) async-start(bf16[8,64,128]{2,1,0:T(8,128)(2,1)} %copy.50), calls=%async_computation.1 | async-start | bytes 262144 | tf_op jit(solution)/shard_map/all_to_all | solution.py:79
  44.9 0.7 copy.45
  45.6 6.0 %all-to-all-done.1 = bf16[8,64,128]{2,1,0:T(8,128)(2,1)S(1)} async-done(((bf16[8,64,128]{2,1,0:T(8,128)(2,1)}), bf16[8,64,128]{2,1,0:T(8,128)(2,1)S(1)}, u32[]{:S(2)}, u32[]{:S(2)}) %all-to-all-start.1) | async-done | bytes 131104 | tf_op jit(solution)/shard_map/all_to_all | solution.py:79
  51.6 3.4 %all-to-all-start = ((bf16[8,64,128]{2,1,0:T(8,128)(2,1)}), bf16[8,64,128]{2,1,0:T(8,128)(2,1)S(1)}, u32[]{:S(2)}, u32[]{:S(2)}) async-start(bf16[8,64,128]{2,1,0:T(8,128)(2,1)} %copy.45), calls=%async_computation | async-start | bytes 262144 | tf_op jit(solution)/shard_map/all_to_all | solution.py:72
  55.9 6.4 %all-to-all-done = bf16[8,64,128]{2,1,0:T(8,128)(2,1)S(1)} async-done(((bf16[8,64,128]{2,1,0:T(8,128)(2,1)}), bf16[8,64,128]{2,1,0:T(8,128)(2,1)S(1)}, u32[]{:S(2)}, u32[]{:S(2)}) %all-to-all-start) | async-done | bytes 131104 | tf_op jit(solution)/shard_map/all_to_all | solution.py:72
  62.5 3.2 %fusion.68 = bf16[64,1024,1]{1,0,2:T(8,128)(2,1)S(1)} fusion(bf16[1024,1024]{1,0:T(8,128)(2,1)} %all-gather.4.cloned.1.call-done, f32[64,1024]{1,0:T(8,128)S(1)} %fusion.16, bf16[1,7,1024,128]{3,2,1,0:T(8,128)(2,1)} %param.11, bf16[64,1024]{1,0:T(8,128)(2,1)S(1)} %copy-done.2, bf16[7,64,128]{2,0,1:T(8,128)(2,1)S(1)} %convolution_convert_fusion.9), kind=kOutput, calls=%fused_computation.45 | convolution fusion | flops 251985920 | bytes 4571136 | tf_op jit(solution)/shard_map/dot_general | solution.py:52
  65.7 1.9 %fusion.84 = bf16[7,64,128]{2,1,0:T(8,128)(2,1)S(1)} fusion(bf16[64,1024,1]{1,0,2:T(8,128)(2,1)S(1)} %fusion.68, bf16[1,7,1024,128]{3,2,1,0:T(8,128)(2,1)} %param.11), kind=kOutput, calls=%fused_computation.56 | convolution fusion | flops 117497856 | bytes 2080768 | tf_op jit(solution)/shard_map/cb,kbr->kcr/dot_general | solution.py:60
  68.2 0.7 copy.60
  68.9 3.4 %all-to-all-start.3 = ((bf16[8,64,128]{2,1,0:T(8,128)(2,1)}), bf16[8,64,128]{2,1,0:T(8,128)(2,1)S(1)}, u32[]{:S(2)}, u32[]{:S(2)}) async-start(bf16[8,64,128]{2,1,0:T(8,128)(2,1)} %copy.60), calls=%async_computation.3 | async-start | bytes 262144 | tf_op jit(solution)/shard_map/all_to_all | solution.py:79
  72.6 0.7 copy.55
  73.3 6.3 %all-to-all-done.3 = bf16[8,64,128]{2,1,0:T(8,128)(2,1)S(1)} async-done(((bf16[8,64,128]{2,1,0:T(8,128)(2,1)}), bf16[8,64,128]{2,1,0:T(8,128)(2,1)S(1)}, u32[]{:S(2)}, u32[]{:S(2)}) %all-to-all-start.3) | async-done | bytes 131104 | tf_op jit(solution)/shard_map/all_to_all | solution.py:79
  79.6 3.4 %all-to-all-start.2 = ((bf16[8,64,128]{2,1,0:T(8,128)(2,1)}), bf16[8,64,128]{2,1,0:T(8,128)(2,1)S(1)}, u32[]{:S(2)}, u32[]{:S(2)}) async-start(bf16[8,64,128]{2,1,0:T(8,128)(2,1)} %copy.55), calls=%async_computation.2 | async-start | bytes 262144 | tf_op jit(solution)/shard_map/all_to_all | solution.py:72
  83.2 0.7 fusion.19
  83.9 6.4 %all-to-all-done.2 = bf16[8,64,128]{2,1,0:T(8,128)(2,1)S(1)} async-done(((bf16[8,64,128]{2,1,0:T(8,128)(2,1)}), bf16[8,64,128]{2,1,0:T(8,128)(2,1)S(1)}, u32[]{:S(2)}, u32[]{:S(2)}) %all-to-all-start.2) | async-done | bytes 131104 | tf_op jit(solution)/shard_map/all_to_all | solution.py:72
  90.5 3.2 %convolution_convert_fusion = bf16[64,1024]{1,0:T(8,128)(2,1)S(1)} fusion(bf16[1024,1024]{1,0:T(8,128)(2,1)} %all-gather.4.cloned.1.call-done, f32[64,1024]{1,0:T(8,128)S(1)} %fusion.19, bf16[1,7,1024,128]{3,2,1,0:T(8,128)(2,1)} %param.11, bf16[64,1024]{1,0:T(8,128)(2,1)S(1)} %copy-done.2, bf16[7,64,128]{2,0,1:T(8,128)(2,1)S(1)} %convolution_convert_fusion.5), kind=kOutput, calls=%fused_computation.30 | convolution fusion | flops 251985920 | bytes 4571136 | tf_op jit(solution)/shard_map/dot_general | solution.py:52
  93.7 6.5 %all_gather.17 = bf16[256,1024]{1,0:T(8,128)(2,1)S(1)} all-gather(bf16[64,1024]{1,0:T(8,128)(2,1)S(1)} %convolution_convert_fusion), channel_id=1, replica_groups=mesh['tiles'=8,'rhs'=4] {'rhs'}, dimensions={0}, use_global_device_ids=true | all-gather | bytes 655360 | tf_op jit(solution)/shard_map/all_gather | solution.py:92
  100.4 0.7 scatter_custom_fusion.1
  101.2 30.9 %all-gather = f32[256,256]{1,0:T(8,128)S(1)} all-gather(f32[32,256]{1,0:T(8,128)S(1)} %scatter_custom_fusion.1), channel_id=2, replica_groups=mesh['tiles'=8,'rhs'=4] {'tiles'}, dimensions={0}, use_global_device_ids=true | all-gather | bytes 294912 | tf_op jit(solution)/shard_map/all_gather | solution.py:102
  (48 shorter events, 5.7 us)
Async XLA Ops:
  7.2 37.0 %copy-start = (bf16[1,7,1024,128]{3,2,1,0:T(8,128)(2,1)S(1)}, bf16[1,7,1024,128]{3,2,1,0:T(8,128)(2,1)}, u32[]{:S(2)}) copy-start(bf16[1,7,1024,128]{3,2,1,0:T(8,128)(2,1)} %param.12) | copy-start | bytes 5505028
  7.2 28.4 %all-gather.4.cloned.1.call-start = ((), (), s32[]{:S(2)}) async-start(), calls=%async_computation.4 | async-start | bytes 2621440 | tf_op jit(solution)/shard_map/all_gather | solution.py:49
  31.4 3.5 %copy-start.6 = (f32[8,32]{1,0:T(8,128)S(1)}, f32[8,32]{1,0:T(8,128)}, u32[]{:S(2)}) copy-start(f32[8,32]{1,0:T(8,128)} %param.16) | copy-start | bytes 3076
  31.4 3.6 %copy-start.4 = (f32[8,1024]{1,0:T(8,128)S(1)}, f32[8,1024]{1,0:T(8,128)}, u32[]{:S(2)}) copy-start(f32[8,1024]{1,0:T(8,128)} %param.15) | copy-start | bytes 98308
  31.4 3.6 %copy-start.7 = (s32[32]{0:T(128)S(1)}, s32[32]{0:T(128)}, u32[]{:S(2)}) copy-start(s32[32]{0:T(128)} %param.17) | copy-start | bytes 388
  31.4 3.8 %copy-start.8 = (s32[1,7]{1,0:T(1,128)S(1)}, s32[1,7]{1,0:T(1,128)}, u32[]{:S(2)}) copy-start(s32[1,7]{1,0:T(1,128)} %param.14) | copy-start | bytes 88
  31.4 4.2 %copy-start.2 = (bf16[64,1024]{1,0:T(8,128)(2,1)S(1)}, bf16[64,1024]{1,0:T(8,128)(2,1)}, u32[]{:S(2)}) copy-start(bf16[64,1024]{1,0:T(8,128)(2,1)} %param.9) | copy-start | bytes 393220
  35.6 2.2 %copy-start.1 = (bf16[1,7,1024,128]{3,2,1,0:T(8,128)(2,1)S(1)}, bf16[1,7,1024,128]{3,2,1,0:T(8,128)(2,1)}, u32[]{:S(2)}) copy-start(bf16[1,7,1024,128]{3,2,1,0:T(8,128)(2,1)} %param.11) | copy-start | bytes 5505028
  38.3 6.3 %copy-start.5 = (s32[1,7]{1,0:T(1,128)S(1)}, s32[1,7]{1,0:T(1,128)}, u32[]{:S(2)}) copy-start(s32[1,7]{1,0:T(1,128)} %param.13) | copy-start | bytes 88
  39.2 12.4 %all-to-all-start.1 = ((bf16[8,64,128]{2,1,0:T(8,128)(2,1)}), bf16[8,64,128]{2,1,0:T(8,128)(2,1)S(1)}, u32[]{:S(2)}, u32[]{:S(2)}) async-start(bf16[8,64,128]{2,1,0:T(8,128)(2,1)} %copy.50), calls=%async_computation.1 | async-start | bytes 262144 | tf_op jit(solution)/shard_map/all_to_all | solution.py:79
  51.6 10.7 %all-to-all-start = ((bf16[8,64,128]{2,1,0:T(8,128)(2,1)}), bf16[8,64,128]{2,1,0:T(8,128)(2,1)S(1)}, u32[]{:S(2)}, u32[]{:S(2)}) async-start(bf16[8,64,128]{2,1,0:T(8,128)(2,1)} %copy.45), calls=%async_computation | async-start | bytes 262144 | tf_op jit(solution)/shard_map/all_to_all | solution.py:72
  68.9 10.7 %all-to-all-start.3 = ((bf16[8,64,128]{2,1,0:T(8,128)(2,1)}), bf16[8,64,128]{2,1,0:T(8,128)(2,1)S(1)}, u32[]{:S(2)}, u32[]{:S(2)}) async-start(bf16[8,64,128]{2,1,0:T(8,128)(2,1)} %copy.60), calls=%async_computation.3 | async-start | bytes 262144 | tf_op jit(solution)/shard_map/all_to_all | solution.py:79
  79.6 10.7 %all-to-all-start.2 = ((bf16[8,64,128]{2,1,0:T(8,128)(2,1)}), bf16[8,64,128]{2,1,0:T(8,128)(2,1)S(1)}, u32[]{:S(2)}, u32[]{:S(2)}) async-start(bf16[8,64,128]{2,1,0:T(8,128)(2,1)} %copy.55), calls=%async_computation.2 | async-start | bytes 262144 | tf_op jit(solution)/shard_map/all_to_all | solution.py:72
  93.7 39.0 %copy-start.3 = (bf16[64,1024]{1,0:T(8,128)(2,1)}, bf16[64,1024]{1,0:T(8,128)(2,1)S(1)}, u32[]{:S(2)}) copy-start(bf16[64,1024]{1,0:T(8,128)(2,1)S(1)} %convolution_convert_fusion) | copy-start | bytes 393220
Sparse Core Ops, SparseCore 0:
  9.5 25.5 all-gather.3
